TPU v7x, 32 devices: a whole 2x2x4 slice. The times are simulated.
32 devices in a mesh: ens: 2 (over x), band: 16 (over z, y, core).
Axes of the slice: x: 2, y: 2, z: 4, core: 2. Of those that a mesh axis runs over, the one named last changes fastest.
Arguments:
- atm_state: bfloat16 [256, 128, 384], P(('ens', 'band')), parts along dimension 0, may hold values from -6 to 6
- ocean_state: bfloat16 [256, 128, 384], P(('ens', 'band')), parts along dimension 0, may hold values from -6 to 6
- dw_kernel: float32 [2, 7, 7, 384], replicated, may hold values from -0.875 to 0.875
- norm_gain: float32 [2, 384], replicated, may hold values from 0.1 to 1.9
- w_up: bfloat16 [2, 384, 1536], replicated, may hold values from -0.3125 to 0.3125
- b_up: float32 [2, 1536], replicated, may hold values from -3 to 3
- w_down: bfloat16 [2, 384, 1536], replicated, may hold values from -0.15625 to 0.15625
- flux_out: bfloat16 [384, 256], replicated, may hold values from -0.3125 to 0.3125
- flux_in: bfloat16 [256, 384], replicated, may hold values from -0.375 to 0.375
- partner: int32 [32], P('ens'), parts along dimension 0, may hold values from 0 to 15, each once
- remap: int32 [256], P('ens'), parts along dimension 0, may hold values from 0 to 7
- land_mask: int32 [256, 128], P(('ens', 'band')), parts along dimension 0, may hold values 0 or 1
Outputs:
- atm_next: bfloat16 [256, 128, 384], P(('ens', 'band')), parts along dimension 0
- ocean_next: bfloat16 [256, 128, 384], P(('ens', 'band')), parts along dimension 0
There are 2 independent parts, one for each index of `ens`. A program takes and returns all parts, laid end to end along the dimension named above; an argument that names none is the same for every part. Nothing has to cross between parts.
Inputs may be any that keep to these rules, and one draw needn't show every extreme that they name: Each of the 16 atmosphere bands is the partner of exactly one ocean band.
All inputs are finite; a program needn't handle non-finite values. No bound on the sum of `land_mask` on one device may be relied on, other than what follows from the above.
Results may differ from a plain program's by a relative error of at most 0.0075.
Values may be sent and summed in bfloat16 or wider, within the bound.
No kernel may reach another device: no remote copies, remote signals or barrier semaphores. Data moves between devices by JAX's collectives and lax.ppermute only.
A program may use at most 64 MiB of HBM per device.

v0:
```python
import jax
import jax.numpy as jnp
from jax import lax
from jax.sharding import PartitionSpec as P


def with_halo(array, sides, width):
    for axis, dim in sides:
        size, length = (lax.axis_size(axis), array.shape[dim])
        up = [(i, (i + 1) % size) for i in range(size - 1)]
        down = [(j, i) for i, j in up]
        last = lax.slice_in_dim(array, length - width, length, axis=dim)
        first = lax.slice_in_dim(array, 0, width, axis=dim)
        before = lax.ppermute(last, axis, up)
        after = lax.ppermute(first, axis, down)
        array = jnp.concatenate([before, array, after], axis=dim)
    return array


def conv_norm(field, kernel, gain):
    padded = with_halo(field, (("band", 0),), 3)
    padded = jnp.concatenate([padded[:, -3:], padded, padded[:, :3]], axis=1).astype(jnp.float32)
    height, width = (field.shape[0], field.shape[1])
    total = jnp.zeros(field.shape, jnp.float32)
    for a in range(7):
        for b in range(7):
            total = total + kernel[a, b] * padded[a : a + height, b : b + width]
    center = jnp.mean(total, axis=-1, keepdims=True)
    spread = jnp.mean((total - center) ** 2, axis=-1, keepdims=True)
    normed = ((total - center) * lax.rsqrt(spread + 1e-06) * gain).astype(jnp.bfloat16)
    return normed.reshape(height * width, field.shape[2])


def mixer(field, which, dw_kernel, norm_gain, w_up, b_up, w_down):
    normed = conv_norm(field, dw_kernel[which], norm_gain[which])
    hidden = jax.nn.gelu(
        jnp.dot(normed, w_up[which], preferred_element_type=jnp.float32) + b_up[which],
        approximate=True,
    ).astype(jnp.bfloat16)
    update = lax.dot_general(
        hidden, w_down[which], (((1,), (1,)), ((), ())), preferred_element_type=jnp.float32
    )
    return (field.astype(jnp.float32) + update.reshape(field.shape)).astype(jnp.bfloat16)


def partner_move(tile, indices):
    picked = jnp.take(
        lax.all_to_all(tile, "band", split_axis=1, concat_axis=0, tiled=True), indices, axis=0
    )
    return lax.all_to_all(picked, "band", split_axis=0, concat_axis=1, tiled=True)


def per_device(
    atm_state,
    ocean_state,
    dw_kernel,
    norm_gain,
    w_up,
    b_up,
    w_down,
    flux_out,
    flux_in,
    partner,
    remap,
    land_mask,
):
    atm_next = mixer(atm_state, 0, dw_kernel, norm_gain, w_up, b_up, w_down)
    height, width, channels = atm_next.shape
    band_rows = remap.shape[0] // partner.shape[0]
    indices = jnp.repeat(partner, band_rows) * band_rows + remap
    surface = jnp.dot(
        atm_next.reshape(-1, channels), flux_out, preferred_element_type=jnp.float32
    ).astype(jnp.bfloat16)
    moved = partner_move(surface.reshape(height, width, -1), indices).reshape(height * width, -1)
    forcing = jnp.dot(moved, flux_in, preferred_element_type=jnp.float32).reshape(
        height, width, channels
    )
    ocean_in = (
        ocean_state.astype(jnp.float32) + land_mask.astype(jnp.float32)[:, :, None] * forcing
    ).astype(jnp.bfloat16)
    ocean_next = mixer(ocean_in, 1, dw_kernel, norm_gain, w_up, b_up, w_down)
    return (atm_next, ocean_next)


def solution(mesh):
    in_specs = (
        P(("ens", "band"), None, None),
        P(("ens", "band"), None, None),
        P(),
        P(),
        P(),
        P(),
        P(),
        P(),
        P(),
        P("ens"),
        P("ens"),
        P(("ens", "band"), None),
    )
    out_specs = (P(("ens", "band"), None, None), P(("ens", "band"), None, None))
    return jax.shard_map(
        per_device, mesh=mesh, in_specs=in_specs, out_specs=out_specs, check_vma=False
    )
```

profile of v0, /device:TPU:13, one launch (start us, length us, event | category | flops | bytes accessed | tf_op | source)
XLA Modules:
  0.0 111.3 jit_solution(1870685209608916670)
XLA Ops:
  0.7 1.2 %fusion.132 = (bf16[3,128,384]{2,1,0:T(8,128)(2,1)S(1)}, bf16[3,128,384]{2,1,0:T(8,128)(2,1)S(1)}) fusion(bf16[8,128,384]{2,1,0:T(8,128)(2,1)} %param.12), kind=kLoop, calls=%fused_computation.360 | loop fusion | bytes 1179648 | tf_op jit(solution)/shard_map/slice | solution.py:13
  1.9 2.6 %collective-permute-start.1 = (bf16[3,128,384]{2,1,0:T(8,128)(2,1)S(1)}, bf16[3,128,384]{2,1,0:T(8,128)(2,1)S(1)}, u32[]{:S(2)}, u32[]{:S(2)}) collective-permute-start(bf16[3,128,384]{2,1,0:T(8,128)(2,1)S(1)} %get-tuple-element.114), channel_id=1, source_target_pairs={{1,0},{2,1},{3,2},{4,3},{5,4},{6,5},{7,6},{8,7},{9,8},{10,9},{11,1... | collective-permute-start | bytes 884744 | tf_op jit(solution)/shard_map/ppermute | solution.py:15
  4.5 3.9 %collective-permute-start = (bf16[3,128,384]{2,1,0:T(8,128)(2,1)S(1)}, bf16[3,128,384]{2,1,0:T(8,128)(2,1)S(1)}, u32[]{:S(2)}, u32[]{:S(2)}) collective-permute-start(bf16[3,128,384]{2,1,0:T(8,128)(2,1)S(1)} %get-tuple-element.115), channel_id=1, source_target_pairs={{0,1},{1,2},{2,3},{3,4},{4,5},{5,6},{6,7},{7,8},{8,9},{9,10},{10,1... | collective-permute-start | bytes 884744 | tf_op jit(solution)/shard_map/ppermute | solution.py:14
  8.3 1.1 %fusion.133 = (f32[1,7,7,384]{3,0,2,1:T(1,128)S(1)}, f32[1,7,7,384]{3,0,2,1:T(1,128)S(1)}) fusion(f32[2,7,7,384]{3,0,2,1:T(2,128)} %param.14), kind=kLoop, calls=%fused_computation.361 | loop fusion | bytes 301056 | tf_op jit(solution)/shard_map/slice | solution.py:35
  9.9 2.1 %collective-permute-done = bf16[3,128,384]{2,1,0:T(8,128)(2,1)S(1)} collective-permute-done((bf16[3,128,384]{2,1,0:T(8,128)(2,1)S(1)}, bf16[3,128,384]{2,1,0:T(8,128)(2,1)S(1)}, u32[]{:S(2)}, u32[]{:S(2)}) %collective-permute-start) | collective-permute-done | bytes 294944 | tf_op jit(solution)/shard_map/ppermute | solution.py:14
  12.3 0.3 maximum_convert_fusion
  12.6 12.0 %fusion.128 = (f32[8,128]{1,0:T(8,128)S(1)}, f32[8,128,384]{2,1,0:T(8,128)}) fusion(f32[14,134,384]{2,1,0:T(8,128)S(1)} %maximum_convert_fusion, f32[384]{0:T(512)S(1)} %get-tuple-element.52, f32[384]{0:T(512)S(1)} %get-tuple-element.53, f32[384]{0:T(512)S(1)} %get-tuple-element.54, f32[384]{0:T(512)S(1)} %get-tuple-element.55, ...), kind=kLoop, calls=%fused_computation.357 | loop fusion | flops 38534144 | bytes 78722560 | tf_op jit(solution)/shard_map/reduce_sum | solution.py:28
  24.6 1.9 %multiply_reduce_fusion.1 = f32[8,128]{1,0:T(8,128)S(1)} fusion(f32[8,128,384]{2,1,0:T(8,128)} %get-tuple-element.109, f32[8,128]{1,0:T(8,128)S(1)} %broadcast_multiply_fusion.1), kind=kLoop, calls=%fused_computation.219 | loop fusion | flops 1178624 | bytes 1581056 | tf_op jit(solution)/shard_map/reduce_sum | solution.py:29
  26.6 0.3 multiply_convert_fusion.1
  26.9 1.3 %copy-done.13 = bf16[2,384,1536]{2,1,0:T(8,128)(2,1)S(1)} copy-done((bf16[2,384,1536]{2,1,0:T(8,128)(2,1)S(1)}, bf16[2,384,1536]{2,1,0:T(8,128)(2,1)}, u32[]{:S(2)}) %copy-start.13) | copy-done | bytes 2359320
  28.2 2.9 %fusion.7 = bf16[1024,1536]{1,0:T(8,128)(2,1)S(1)} fusion(bf16[1024,384]{1,0:T(8,128)(2,1)S(1)} %bitcast.48, f32[1536]{0:T(1024)S(1)} %get-tuple-element.101, bf16[2,384,1536]{2,1,0:T(8,128)(2,1)S(1)} %copy-done.13), kind=kOutput, calls=%fused_computation.10 | convolution fusion | flops 1223688192 | bytes 5120000 | tf_op jit(solution)/shard_map/dot_general | solution.py:37
  31.1 1.8 %add_convert_fusion.2 = bf16[8,128,384]{2,1,0:T(8,128)(2,1)S(1)} fusion(bf16[8,128,384]{2,1,0:T(8,128)(2,1)S(1)} %copy-done.6, bf16[8,128,1536]{2,1,0:T(8,128)(2,1)S(1)} %bitcast.51, bf16[2,384,1536]{2,1,0:T(8,128)(2,1)S(1)} %copy-done.15), kind=kOutput, calls=%fused_computation.217 | convolution fusion | flops 1209139200 | bytes 5898240 | tf_op jit(solution)/shard_map/dot_general | solution.py:40
  33.0 0.9 copy-done.7
  33.8 0.4 convolution_convert_fusion
  34.3 1.1 copy.22
  35.4 7.5 %all-to-all-start = ((bf16[8,128,256]{2,0,1:T(8,128)(2,1)}), bf16[8,128,256]{2,0,1:T(8,128)(2,1)S(1)}, u32[]{:S(2)}, u32[]{:S(2)}) async-start(bf16[8,128,256]{2,0,1:T(8,128)(2,1)} %copy.22), calls=%async_computation | async-start | bytes 1048576 | tf_op jit(solution)/shard_map/all_to_all | solution.py:48
  43.1 13.4 %all-to-all-done = bf16[8,128,256]{2,0,1:T(8,128)(2,1)S(1)} async-done(((bf16[8,128,256]{2,0,1:T(8,128)(2,1)}), bf16[8,128,256]{2,0,1:T(8,128)(2,1)S(1)}, u32[]{:S(2)}, u32[]{:S(2)}) %all-to-all-start) | async-done | bytes 524320 | tf_op jit(solution)/shard_map/all_to_all | solution.py:48
  56.6 0.6 gather_fusion
  57.2 1.0 broadcast_select_fusion
  58.2 4.9 %all-to-all-start.1 = ((bf16[128,8,256]{2,1,0:T(8,128)(2,1)}), bf16[128,8,256]{2,1,0:T(8,128)(2,1)S(1)}, u32[]{:S(2)}, u32[]{:S(2)}) async-start(bf16[128,8,256]{2,1,0:T(8,128)(2,1)} %broadcast_select_fusion), calls=%async_computation.1 | async-start | bytes 1048576 | tf_op jit(solution)/shard_map/all_to_all | solution.py:50
  63.1 13.6 %all-to-all-done.1 = bf16[128,8,256]{2,1,0:T(8,128)(2,1)S(1)} async-done(((bf16[128,8,256]{2,1,0:T(8,128)(2,1)}), bf16[128,8,256]{2,1,0:T(8,128)(2,1)S(1)}, u32[]{:S(2)}, u32[]{:S(2)}) %all-to-all-start.1) | async-done | bytes 524320 | tf_op jit(solution)/shard_map/all_to_all | solution.py:50
  76.7 0.4 add_convert_fusion.1
  77.2 3.7 %collective-permute-start.2 = (bf16[3,128,384]{2,1,0:T(8,128)(2,1)S(1)}, bf16[3,128,384]{2,1,0:T(8,128)(2,1)S(1)}, u32[]{:S(2)}, u32[]{:S(2)}) collective-permute-start(bf16[3,128,384]{2,1,0:T(8,128)(2,1)S(1)} %get-tuple-element.112), channel_id=1, source_target_pairs={{0,1},{1,2},{2,3},{3,4},{4,5},{5,6},{6,7},{7,8},{8,9},{9,10},{10,1... | collective-permute-start | bytes 884744 | tf_op jit(solution)/shard_map/ppermute | solution.py:14
  80.9 2.1 %collective-permute-start.3 = (bf16[3,128,384]{2,1,0:T(8,128)(2,1)S(1)}, bf16[3,128,384]{2,1,0:T(8,128)(2,1)S(1)}, u32[]{:S(2)}, u32[]{:S(2)}) collective-permute-start(bf16[3,128,384]{2,1,0:T(8,128)(2,1)S(1)} %get-tuple-element.113), channel_id=1, source_target_pairs={{1,0},{2,1},{3,2},{4,3},{5,4},{6,5},{7,6},{8,7},{9,8},{10,9},{11,1... | collective-permute-start | bytes 884744 | tf_op jit(solution)/shard_map/ppermute | solution.py:15
  83.2 1.3 %collective-permute-done.2 = bf16[3,128,384]{2,1,0:T(8,128)(2,1)S(1)} collective-permute-done((bf16[3,128,384]{2,1,0:T(8,128)(2,1)S(1)}, bf16[3,128,384]{2,1,0:T(8,128)(2,1)S(1)}, u32[]{:S(2)}, u32[]{:S(2)}) %collective-permute-start.2) | collective-permute-done | bytes 294944 | tf_op jit(solution)/shard_map/ppermute | solution.py:14
  84.6 5.3 %collective-permute-done.3 = bf16[3,128,384]{2,1,0:T(8,128)(2,1)S(1)} collective-permute-done((bf16[3,128,384]{2,1,0:T(8,128)(2,1)S(1)}, bf16[3,128,384]{2,1,0:T(8,128)(2,1)S(1)}, u32[]{:S(2)}, u32[]{:S(2)}) %collective-permute-start.3) | collective-permute-done | bytes 294944 | tf_op jit(solution)/shard_map/ppermute | solution.py:15
  90.2 12.0 %fusion.126 = (f32[8,128]{1,0:T(8,128)S(1)}, f32[8,128,384]{2,1,0:T(8,128)}) fusion(f32[14,134,384]{2,1,0:T(8,128)S(1)} %fusion.113, f32[384]{0:T(512)S(1)} %get-tuple-element.3, f32[384]{0:T(512)S(1)} %get-tuple-element.4, f32[384]{0:T(512)S(1)} %get-tuple-element.5, f32[384]{0:T(512)S(1)} %get-tuple-element.6, f32[384]{0:T(512)S(1)} %get-tuple-element.7, ...), kind=kLoop, calls=%fused_computation.356 | loop fusion | flops 38534144 | bytes 78722560 | tf_op jit(solution)/shard_map/reduce_sum | solution.py:28
  102.1 1.9 %multiply_reduce_fusion = f32[8,128]{1,0:T(8,128)S(1)} fusion(f32[8,128,384]{2,1,0:T(8,128)} %get-tuple-element.105, f32[8,128]{1,0:T(8,128)S(1)} %broadcast_multiply_fusion), kind=kLoop, calls=%fused_computation.215 | loop fusion | flops 1178624 | bytes 1581056 | tf_op jit(solution)/shard_map/reduce_sum | solution.py:29
  104.1 0.3 multiply_convert_fusion
  104.4 1.3 %copy-done.14 = bf16[2,384,1536]{2,1,0:T(8,128)(2,1)S(1)} copy-done((bf16[2,384,1536]{2,1,0:T(8,128)(2,1)S(1)}, bf16[2,384,1536]{2,1,0:T(8,128)(2,1)}, u32[]{:S(2)}) %copy-start.14) | copy-done | bytes 2359320
  105.7 2.9 %fusion.15 = bf16[1024,1536]{1,0:T(8,128)(2,1)S(1)} fusion(bf16[1024,384]{1,0:T(8,128)(2,1)S(1)} %bitcast.47, f32[1536]{0:T(1024)S(1)} %get-tuple-element.100, bf16[2,384,1536]{2,1,0:T(8,128)(2,1)S(1)} %copy-done.14), kind=kOutput, calls=%fused_computation.18 | convolution fusion | flops 1223688192 | bytes 5120000 | tf_op jit(solution)/shard_map/dot_general | solution.py:37
  108.6 2.7 %add_convert_fusion = bf16[8,128,384]{2,1,0:T(8,128)(2,1)} fusion(bf16[8,128,384]{2,1,0:T(8,128)(2,1)S(1)} %copy-done.4, bf16[8,128,1536]{2,1,0:T(8,128)(2,1)S(1)} %bitcast.50, bf16[2,384,1536]{2,1,0:T(8,128)(2,1)S(1)} %copy-done.16), kind=kOutput, calls=%fused_computation.213 | convolution fusion | flops 1209139200 | bytes 5898240 | tf_op jit(solution)/shard_map/dot_general | solution.py:40
  (62 shorter events, 1.7 us)
Async XLA Ops:
  0.6 76.0 %copy-start = (bf16[256,384]{1,0:T(8,128)(2,1)S(1)}, bf16[256,384]{1,0:T(8,128)(2,1)}, u32[]{:S(2)}) copy-start(bf16[256,384]{1,0:T(8,128)(2,1)} %param.20) | copy-start | bytes 589828
  0.6 11.4 %copy-start.5 = (bf16[8,128,384]{2,1,0:T(8,128)(2,1)S(1)}, bf16[8,128,384]{2,1,0:T(8,128)(2,1)}, u32[]{:S(2)}) copy-start(bf16[8,128,384]{2,1,0:T(8,128)(2,1)} %param.12) | copy-start | bytes 2359300
  0.7 9.0 %copy-start.9 = (f32[2,1536]{1,0:T(2,128)S(1)}, f32[2,1536]{1,0:T(2,128)}, u32[]{:S(2)}) copy-start(f32[2,1536]{1,0:T(2,128)} %param.17) | copy-start | bytes 36868
  0.7 9.2 %copy-start.11 = (f32[2,384]{1,0:T(2,128)S(1)}, f32[2,384]{1,0:T(2,128)}, u32[]{:S(2)}) copy-start(f32[2,384]{1,0:T(2,128)} %param.15) | copy-start | bytes 9220
  1.9 10.3 %collective-permute-start.1 = (bf16[3,128,384]{2,1,0:T(8,128)(2,1)S(1)}, bf16[3,128,384]{2,1,0:T(8,128)(2,1)S(1)}, u32[]{:S(2)}, u32[]{:S(2)}) collective-permute-start(bf16[3,128,384]{2,1,0:T(8,128)(2,1)S(1)} %get-tuple-element.114), channel_id=1, source_target_pairs={{1,0},{2,1},{3,2},{4,3},{5,4},{6,5},{7,6},{8,7},{9,8},{10,9},{11,1... | collective-permute-start | bytes 884744 | tf_op jit(solution)/shard_map/ppermute | solution.py:15
  4.5 7.5 %collective-permute-start = (bf16[3,128,384]{2,1,0:T(8,128)(2,1)S(1)}, bf16[3,128,384]{2,1,0:T(8,128)(2,1)S(1)}, u32[]{:S(2)}, u32[]{:S(2)}) collective-permute-start(bf16[3,128,384]{2,1,0:T(8,128)(2,1)S(1)} %get-tuple-element.115), channel_id=1, source_target_pairs={{0,1},{1,2},{2,3},{3,4},{4,5},{5,6},{6,7},{7,8},{8,9},{9,10},{10,1... | collective-permute-start | bytes 884744 | tf_op jit(solution)/shard_map/ppermute | solution.py:14
  24.6 1.9 %copy-start.2 = (f32[8,128,384]{2,1,0:T(8,128)S(1)}, f32[8,128,384]{2,1,0:T(8,128)}, u32[]{:S(2)}) copy-start(f32[8,128,384]{2,1,0:T(8,128)} %get-tuple-element.109) | copy-start | bytes 4718596
  26.5 1.7 %copy-start.13 = (bf16[2,384,1536]{2,1,0:T(8,128)(2,1)S(1)}, bf16[2,384,1536]{2,1,0:T(8,128)(2,1)}, u32[]{:S(2)}) copy-start(bf16[2,384,1536]{2,1,0:T(8,128)(2,1)} %param.16) | copy-start | bytes 7077892
  28.2 2.9 %copy-start.6 = (bf16[8,128,384]{2,1,0:T(8,128)(2,1)S(1)}, bf16[8,128,384]{2,1,0:T(8,128)(2,1)}, u32[]{:S(2)}) copy-start(bf16[8,128,384]{2,1,0:T(8,128)(2,1)} %param.12) | copy-start | bytes 2359300
  28.2 2.9 %copy-start.15 = (bf16[2,384,1536]{2,1,0:T(8,128)(2,1)S(1)}, bf16[2,384,1536]{2,1,0:T(8,128)(2,1)}, u32[]{:S(2)}) copy-start(bf16[2,384,1536]{2,1,0:T(8,128)(2,1)} %param.18) | copy-start | bytes 7077892
  31.1 2.7 %copy-start.8 = (bf16[384,256]{1,0:T(8,128)(2,1)S(1)}, bf16[384,256]{1,0:T(8,128)(2,1)}, u32[]{:S(2)}) copy-start(bf16[384,256]{1,0:T(8,128)(2,1)} %param.19) | copy-start | bytes 589828
  32.9 0.9 copy-start.7
  33.8 9.0 %copy-start.18 = (s32[16]{0:T(128)S(1)}, s32[16]{0:T(128)}, u32[]{:S(2)}) copy-start(s32[16]{0:T(128)} %param.21) | copy-start | bytes 196
  33.8 9.2 %copy-start.12 = (s32[128]{0:T(128)S(1)}, s32[128]{0:T(128)}, u32[]{:S(2)}) copy-start(s32[128]{0:T(128)} %param.22) | copy-start | bytes 1540
  35.4 21.1 %all-to-all-start = ((bf16[8,128,256]{2,0,1:T(8,128)(2,1)}), bf16[8,128,256]{2,0,1:T(8,128)(2,1)S(1)}, u32[]{:S(2)}, u32[]{:S(2)}) async-start(bf16[8,128,256]{2,0,1:T(8,128)(2,1)} %copy.22), calls=%async_computation | async-start | bytes 1048576 | tf_op jit(solution)/shard_map/all_to_all | solution.py:48
  56.5 6.5 %copy-start.10 = (s32[8,128]{1,0:T(8,128)S(1)}, s32[8,128]{1,0:T(8,128)}, u32[]{:S(2)}) copy-start(s32[8,128]{1,0:T(8,128)} %param.23) | copy-start | bytes 12292
  56.6 20.1 %copy-start.17 = (bf16[8,128,384]{2,1,0:T(8,128)(2,1)S(1)}, bf16[8,128,384]{2,1,0:T(8,128)(2,1)}, u32[]{:S(2)}) copy-start(bf16[8,128,384]{2,1,0:T(8,128)(2,1)} %param.13) | copy-start | bytes 2359300
  58.2 18.4 %all-to-all-start.1 = ((bf16[128,8,256]{2,1,0:T(8,128)(2,1)}), bf16[128,8,256]{2,1,0:T(8,128)(2,1)S(1)}, u32[]{:S(2)}, u32[]{:S(2)}) async-start(bf16[128,8,256]{2,1,0:T(8,128)(2,1)} %broadcast_select_fusion), calls=%async_computation.1 | async-start | bytes 1048576 | tf_op jit(solution)/shard_map/all_to_all | solution.py:50
  77.1 13.0 %copy-start.3 = (bf16[8,128,384]{2,1,0:T(8,128)(2,1)}, bf16[8,128,384]{2,1,0:T(8,128)(2,1)S(1)}, u32[]{:S(2)}) copy-start(bf16[8,128,384]{2,1,0:T(8,128)(2,1)S(1)} %add_convert_fusion.1) | copy-start | bytes 2359300
  77.2 7.4 %collective-permute-start.2 = (bf16[3,128,384]{2,1,0:T(8,128)(2,1)S(1)}, bf16[3,128,384]{2,1,0:T(8,128)(2,1)S(1)}, u32[]{:S(2)}, u32[]{:S(2)}) collective-permute-start(bf16[3,128,384]{2,1,0:T(8,128)(2,1)S(1)} %get-tuple-element.112), channel_id=1, source_target_pairs={{0,1},{1,2},{2,3},{3,4},{4,5},{5,6},{6,7},{7,8},{8,9},{9,10},{10,1... | collective-permute-start | bytes 884744 | tf_op jit(solution)/shard_map/ppermute | solution.py:14
  80.9 8.9 %collective-permute-start.3 = (bf16[3,128,384]{2,1,0:T(8,128)(2,1)S(1)}, bf16[3,128,384]{2,1,0:T(8,128)(2,1)S(1)}, u32[]{:S(2)}, u32[]{:S(2)}) collective-permute-start(bf16[3,128,384]{2,1,0:T(8,128)(2,1)S(1)} %get-tuple-element.113), channel_id=1, source_target_pairs={{1,0},{2,1},{3,2},{4,3},{5,4},{6,5},{7,6},{8,7},{9,8},{10,9},{11,1... | collective-permute-start | bytes 884744 | tf_op jit(solution)/shard_map/ppermute | solution.py:15
  102.1 1.9 %copy-start.1 = (f32[8,128,384]{2,1,0:T(8,128)S(1)}, f32[8,128,384]{2,1,0:T(8,128)}, u32[]{:S(2)}) copy-start(f32[8,128,384]{2,1,0:T(8,128)} %get-tuple-element.105) | copy-start | bytes 4718596
  104.0 1.7 %copy-start.14 = (bf16[2,384,1536]{2,1,0:T(8,128)(2,1)S(1)}, bf16[2,384,1536]{2,1,0:T(8,128)(2,1)}, u32[]{:S(2)}) copy-start(bf16[2,384,1536]{2,1,0:T(8,128)(2,1)} %param.16) | copy-start | bytes 7077892
  105.7 2.9 %copy-start.4 = (bf16[8,128,384]{2,1,0:T(8,128)(2,1)S(1)}, bf16[8,128,384]{2,1,0:T(8,128)(2,1)}, u32[]{:S(2)}) copy-start(bf16[8,128,384]{2,1,0:T(8,128)(2,1)} %copy-done.3) | copy-start | bytes 2359300
  105.7 2.9 %copy-start.16 = (bf16[2,384,1536]{2,1,0:T(8,128)(2,1)S(1)}, bf16[2,384,1536]{2,1,0:T(8,128)(2,1)}, u32[]{:S(2)}) copy-start(bf16[2,384,1536]{2,1,0:T(8,128)(2,1)} %param.18) | copy-start | bytes 7077892
where the time goes:
time: 112 us; the launch traced here: 111 us
  waiting for transfers between devices  35.6 us (32%)
  other arithmetic  30.1 us (27%)
  starting transfers between devices  24.6 us (22%)
  matrix products  11.2 us (10%)
  local copies, waits for them, and re-layouts  8.78 us (8%)
    reduce_sum x2, other arithmetic, conv_norm(): center = jnp.mean(total, axis=-1, keepdims=True)  23.9 us
    all_to_all x1, waiting for transfers between devices, partner_move(): lax.all_to_all(picked, 'band', split_axis=0, concat_axis=1, tiled=True)  13.6 us
    all_to_all x1, waiting for transfers between devices, partner_move(): lax.all_to_all(tile, 'band', split_axis=1, concat_axis=0, tiled=True)  13.4 us
    ppermute x2, starting transfers between devices, with_halo(): before = lax.ppermute(last, axis, up)  7.54 us
    all_to_all x1, starting transfers between devices, partner_move(): lax.all_to_all(tile, 'band', split_axis=1, concat_axis=0, tiled=True)  7.51 us
    dot_general x2, matrix products, mixer(): jnp.dot(normed, w_up[which], preferred_element_type=jnp.float32)  5.77 us
    ppermute x2, waiting for transfers between devices, with_halo(): after = lax.ppermute(first, axis, down)  5.25 us
    all_to_all x1, starting transfers between devices, partner_move(): lax.all_to_all(picked, 'band', split_axis=0, concat_axis=1, tiled=True)  4.87 us
  transfers between devices with their start and end apart: 6, of which 5 were waited for; matrix products, arithmetic and copies ran while one was open for 2% of the time, Pallas kernels for 0%

commit v1 on v0

--- a/solution.py
+++ b/solution.py
@@ -47,7 +47,10 @@
     picked = jnp.take(
         lax.all_to_all(tile, "band", split_axis=1, concat_axis=0, tiled=True), indices, axis=0
     )
-    return lax.all_to_all(picked, "band", split_axis=0, concat_axis=1, tiled=True)
+    return jnp.concatenate(
+        lax.all_to_all(jnp.stack(jnp.split(picked, lax.axis_size("band"), axis=0)), "band", 0, 0),
+        axis=1,
+    )
 
 
 def per_device(

time: 112 us -> 121 us (1.080)
  local copies, waits for them, and re-layouts: 8.78 us -> 18.7 us
    unnamed x40 -> x55, local copies, waits for them, and re-layouts: 3.71 us -> 13 us
where the time goes in v1:
time: 121 us; the launch traced here: 120 us
  waiting for transfers between devices  35.6 us (29%)
  other arithmetic  29.3 us (24%)
  starting transfers between devices  24.6 us (20%)
  local copies, waits for them, and re-layouts  18.7 us (15%)
  matrix products  11.2 us (9%)
    reduce_sum x2, other arithmetic, conv_norm(): center = jnp.mean(total, axis=-1, keepdims=True)  23.9 us
    all_to_all x1, waiting for transfers between devices, partner_move(): lax.all_to_all(jnp.stack(jnp.split(picked, lax.axis_size('band'), axis=0)...  13.6 us
    all_to_all x1, waiting for transfers between devices, partner_move(): lax.all_to_all(tile, 'band', split_axis=1, concat_axis=0, tiled=True)  13.4 us
    unnamed x55, local copies, waits for them, and re-layouts  13 us
    ppermute x2, starting transfers between devices, with_halo(): before = lax.ppermute(last, axis, up)  7.55 us
    all_to_all x1, starting transfers between devices, partner_move(): lax.all_to_all(tile, 'band', split_axis=1, concat_axis=0, tiled=True)  7.51 us
    dot_general x2, matrix products, mixer(): jnp.dot(normed, w_up[which], preferred_element_type=jnp.float32)  5.77 us
    ppermute x2, waiting for transfers between devices, with_halo(): after = lax.ppermute(first, axis, down)  5.25 us
  transfers between devices with their start and end apart: 6, of which 5 were waited for; matrix products, arithmetic and copies ran while one was open for 2% of the time, Pallas kernels for 0%

profile of v1, /device:TPU:13, one launch (start us, length us, event | category | flops | bytes accessed | tf_op | source)
XLA Modules:
  0.0 120.4 jit_solution(7862633904614548391)
XLA Ops:
  0.7 1.2 fusion.132
  1.9 2.6 %collective-permute-start.1 = (bf16[3,128,384]{2,1,0:T(8,128)(2,1)S(1)}, bf16[3,128,384]{2,1,0:T(8,128)(2,1)S(1)}, u32[]{:S(2)}, u32[]{:S(2)}) collective-permute-start(bf16[3,128,384]{2,1,0:T(8,128)(2,1)S(1)} %get-tuple-element.114), channel_id=1, source_target_pairs={{1,0},{2,1},{3,2},{4,3},{5,4},{6,5},{7,6},{8,7},{9,8},{10,9},{11,1... | collective-permute-start | bytes 884744 | tf_op jit(solution)/shard_map/ppermute | solution.py:15
  4.5 3.9 %collective-permute-start = (bf16[3,128,384]{2,1,0:T(8,128)(2,1)S(1)}, bf16[3,128,384]{2,1,0:T(8,128)(2,1)S(1)}, u32[]{:S(2)}, u32[]{:S(2)}) collective-permute-start(bf16[3,128,384]{2,1,0:T(8,128)(2,1)S(1)} %get-tuple-element.115), channel_id=1, source_target_pairs={{0,1},{1,2},{2,3},{3,4},{4,5},{5,6},{6,7},{7,8},{8,9},{9,10},{10,1... | collective-permute-start | bytes 884744 | tf_op jit(solution)/shard_map/ppermute | solution.py:14
  8.3 1.1 fusion.133
  9.9 2.1 %collective-permute-done = bf16[3,128,384]{2,1,0:T(8,128)(2,1)S(1)} collective-permute-done((bf16[3,128,384]{2,1,0:T(8,128)(2,1)S(1)}, bf16[3,128,384]{2,1,0:T(8,128)(2,1)S(1)}, u32[]{:S(2)}, u32[]{:S(2)}) %collective-permute-start) | collective-permute-done | bytes 294944 | tf_op jit(solution)/shard_map/ppermute | solution.py:14
  12.6 12.0 %fusion.128 = (f32[8,128]{1,0:T(8,128)S(1)}, f32[8,128,384]{2,1,0:T(8,128)}) fusion(f32[14,134,384]{2,1,0:T(8,128)S(1)} %maximum_convert_fusion, f32[384]{0:T(512)S(1)} %get-tuple-element.52, f32[384]{0:T(512)S(1)} %get-tuple-element.53, f32[384]{0:T(512)S(1)} %get-tuple-element.54, f32[384]{0:T(512)S(1)} %get-tuple-element.55, ...), kind=kLoop, calls=%fused_computation.389 | loop fusion | flops 38534144 | bytes 78722560 | tf_op jit(solution)/shard_map/reduce_sum | solution.py:28
  24.6 1.9 %multiply_reduce_fusion.1 = f32[8,128]{1,0:T(8,128)S(1)} fusion(f32[8,128,384]{2,1,0:T(8,128)} %get-tuple-element.109, f32[8,128]{1,0:T(8,128)S(1)} %broadcast_multiply_fusion.1), kind=kLoop, calls=%fused_computation.219 | loop fusion | flops 1178624 | bytes 1581056 | tf_op jit(solution)/shard_map/reduce_sum | solution.py:29
  26.9 1.3 %copy-done.13 = bf16[2,384,1536]{2,1,0:T(8,128)(2,1)S(1)} copy-done((bf16[2,384,1536]{2,1,0:T(8,128)(2,1)S(1)}, bf16[2,384,1536]{2,1,0:T(8,128)(2,1)}, u32[]{:S(2)}) %copy-start.13) | copy-done | bytes 2359320
  28.2 2.9 %fusion.7 = bf16[1024,1536]{1,0:T(8,128)(2,1)S(1)} fusion(bf16[1024,384]{1,0:T(8,128)(2,1)S(1)} %bitcast.113, f32[1536]{0:T(1024)S(1)} %get-tuple-element.101, bf16[2,384,1536]{2,1,0:T(8,128)(2,1)S(1)} %copy-done.13), kind=kOutput, calls=%fused_computation.10 | convolution fusion | flops 1223688192 | bytes 5120000 | tf_op jit(solution)/shard_map/dot_general | solution.py:37
  31.1 1.8 %add_convert_fusion.2 = bf16[8,128,384]{2,1,0:T(8,128)(2,1)S(1)} fusion(bf16[8,128,384]{2,1,0:T(8,128)(2,1)S(1)} %copy-done.6, bf16[8,128,1536]{2,1,0:T(8,128)(2,1)S(1)} %bitcast.115, bf16[2,384,1536]{2,1,0:T(8,128)(2,1)S(1)} %copy-done.15), kind=kOutput, calls=%fused_computation.217 | convolution fusion | flops 1209139200 | bytes 5898240 | tf_op jit(solution)/shard_map/dot_general | solution.py:40
  33.0 0.9 copy-done.7
  34.3 1.1 copy.37
  35.4 7.5 %all-to-all-start = ((bf16[8,128,256]{2,0,1:T(8,128)(2,1)}), bf16[8,128,256]{2,0,1:T(8,128)(2,1)S(1)}, u32[]{:S(2)}, u32[]{:S(2)}) async-start(bf16[8,128,256]{2,0,1:T(8,128)(2,1)} %copy.37), calls=%async_computation | async-start | bytes 1048576 | tf_op jit(solution)/shard_map/all_to_all | solution.py:48
  43.1 13.4 %all-to-all-done = bf16[8,128,256]{2,0,1:T(8,128)(2,1)S(1)} async-done(((bf16[8,128,256]{2,0,1:T(8,128)(2,1)}), bf16[8,128,256]{2,0,1:T(8,128)(2,1)S(1)}, u32[]{:S(2)}, u32[]{:S(2)}) %all-to-all-start) | async-done | bytes 524320 | tf_op jit(solution)/shard_map/all_to_all | solution.py:48
  56.5 0.6 gather_fusion
  57.4 0.6 constant_dynamic-update-slice_fusion.18
  58.1 0.6 constant_dynamic-update-slice_fusion.17
  58.7 0.6 constant_dynamic-update-slice_fusion.16
  59.3 0.6 constant_dynamic-update-slice_fusion.15
  59.9 0.6 constant_dynamic-update-slice_fusion.14
  60.5 0.6 constant_dynamic-update-slice_fusion.13
  67.3 4.9 %all-to-all-start.1 = ((bf16[16,8,8,256]{3,2,1,0:T(8,128)(2,1)}), bf16[16,8,8,256]{3,2,1,0:T(8,128)(2,1)S(1)}, u32[]{:S(2)}, u32[]{:S(2)}) async-start(bf16[16,8,8,256]{3,2,1,0:T(8,128)(2,1)} %constant_dynamic-update-slice_fusion.3), calls=%async_computation.1 | async-start | bytes 1048576 | tf_op jit(solution)/shard_map/all_to_all | solution.py:51
  72.2 13.6 %all-to-all-done.1 = bf16[16,8,8,256]{3,2,1,0:T(8,128)(2,1)S(1)} async-done(((bf16[16,8,8,256]{3,2,1,0:T(8,128)(2,1)}), bf16[16,8,8,256]{3,2,1,0:T(8,128)(2,1)S(1)}, u32[]{:S(2)}, u32[]{:S(2)}) %all-to-all-start.1) | async-done | bytes 524320 | tf_op jit(solution)/shard_map/all_to_all | solution.py:51
  86.3 3.7 %collective-permute-start.2 = (bf16[3,128,384]{2,1,0:T(8,128)(2,1)S(1)}, bf16[3,128,384]{2,1,0:T(8,128)(2,1)S(1)}, u32[]{:S(2)}, u32[]{:S(2)}) collective-permute-start(bf16[3,128,384]{2,1,0:T(8,128)(2,1)S(1)} %get-tuple-element.112), channel_id=1, source_target_pairs={{0,1},{1,2},{2,3},{3,4},{4,5},{5,6},{6,7},{7,8},{8,9},{9,10},{10,1... | collective-permute-start | bytes 884744 | tf_op jit(solution)/shard_map/ppermute | solution.py:14
  90.0 2.1 %collective-permute-start.3 = (bf16[3,128,384]{2,1,0:T(8,128)(2,1)S(1)}, bf16[3,128,384]{2,1,0:T(8,128)(2,1)S(1)}, u32[]{:S(2)}, u32[]{:S(2)}) collective-permute-start(bf16[3,128,384]{2,1,0:T(8,128)(2,1)S(1)} %get-tuple-element.113), channel_id=1, source_target_pairs={{1,0},{2,1},{3,2},{4,3},{5,4},{6,5},{7,6},{8,7},{9,8},{10,9},{11,1... | collective-permute-start | bytes 884744 | tf_op jit(solution)/shard_map/ppermute | solution.py:15
  92.3 1.3 %collective-permute-done.2 = bf16[3,128,384]{2,1,0:T(8,128)(2,1)S(1)} collective-permute-done((bf16[3,128,384]{2,1,0:T(8,128)(2,1)S(1)}, bf16[3,128,384]{2,1,0:T(8,128)(2,1)S(1)}, u32[]{:S(2)}, u32[]{:S(2)}) %collective-permute-start.2) | collective-permute-done | bytes 294944 | tf_op jit(solution)/shard_map/ppermute | solution.py:14
  93.7 5.3 %collective-permute-done.3 = bf16[3,128,384]{2,1,0:T(8,128)(2,1)S(1)} collective-permute-done((bf16[3,128,384]{2,1,0:T(8,128)(2,1)S(1)}, bf16[3,128,384]{2,1,0:T(8,128)(2,1)S(1)}, u32[]{:S(2)}, u32[]{:S(2)}) %collective-permute-start.3) | collective-permute-done | bytes 294944 | tf_op jit(solution)/shard_map/ppermute | solution.py:15
  99.3 12.0 %fusion.126 = (f32[8,128]{1,0:T(8,128)S(1)}, f32[8,128,384]{2,1,0:T(8,128)}) fusion(f32[14,134,384]{2,1,0:T(8,128)S(1)} %fusion.113, f32[384]{0:T(512)S(1)} %get-tuple-element.3, f32[384]{0:T(512)S(1)} %get-tuple-element.4, f32[384]{0:T(512)S(1)} %get-tuple-element.5, f32[384]{0:T(512)S(1)} %get-tuple-element.6, f32[384]{0:T(512)S(1)} %get-tuple-element.7, ...), kind=kLoop, calls=%fused_computation.388 | loop fusion | flops 38534144 | bytes 78722560 | tf_op jit(solution)/shard_map/reduce_sum | solution.py:28
  111.2 1.9 %multiply_reduce_fusion = f32[8,128]{1,0:T(8,128)S(1)} fusion(f32[8,128,384]{2,1,0:T(8,128)} %get-tuple-element.105, f32[8,128]{1,0:T(8,128)S(1)} %broadcast_multiply_fusion), kind=kLoop, calls=%fused_computation.215 | loop fusion | flops 1178624 | bytes 1581056 | tf_op jit(solution)/shard_map/reduce_sum | solution.py:29
  113.5 1.3 %copy-done.14 = bf16[2,384,1536]{2,1,0:T(8,128)(2,1)S(1)} copy-done((bf16[2,384,1536]{2,1,0:T(8,128)(2,1)S(1)}, bf16[2,384,1536]{2,1,0:T(8,128)(2,1)}, u32[]{:S(2)}) %copy-start.14) | copy-done | bytes 2359320
  114.8 2.9 %fusion.15 = bf16[1024,1536]{1,0:T(8,128)(2,1)S(1)} fusion(bf16[1024,384]{1,0:T(8,128)(2,1)S(1)} %bitcast.112, f32[1536]{0:T(1024)S(1)} %get-tuple-element.100, bf16[2,384,1536]{2,1,0:T(8,128)(2,1)S(1)} %copy-done.14), kind=kOutput, calls=%fused_computation.18 | convolution fusion | flops 1223688192 | bytes 5120000 | tf_op jit(solution)/shard_map/dot_general | solution.py:37
  117.7 2.7 %add_convert_fusion = bf16[8,128,384]{2,1,0:T(8,128)(2,1)} fusion(bf16[8,128,384]{2,1,0:T(8,128)(2,1)S(1)} %copy-done.4, bf16[8,128,1536]{2,1,0:T(8,128)(2,1)S(1)} %bitcast.114, bf16[2,384,1536]{2,1,0:T(8,128)(2,1)S(1)} %copy-done.16), kind=kOutput, calls=%fused_computation.213 | convolution fusion | flops 1209139200 | bytes 5898240 | tf_op jit(solution)/shard_map/dot_general | solution.py:40
  (78 shorter events, 9.9 us)
Async XLA Ops:
  0.6 85.1 %copy-start = (bf16[256,384]{1,0:T(8,128)(2,1)S(1)}, bf16[256,384]{1,0:T(8,128)(2,1)}, u32[]{:S(2)}) copy-start(bf16[256,384]{1,0:T(8,128)(2,1)} %param.20) | copy-start | bytes 589828
  0.6 11.4 %copy-start.5 = (bf16[8,128,384]{2,1,0:T(8,128)(2,1)S(1)}, bf16[8,128,384]{2,1,0:T(8,128)(2,1)}, u32[]{:S(2)}) copy-start(bf16[8,128,384]{2,1,0:T(8,128)(2,1)} %param.12) | copy-start | bytes 2359300
  0.7 9.0 %copy-start.9 = (f32[2,1536]{1,0:T(2,128)S(1)}, f32[2,1536]{1,0:T(2,128)}, u32[]{:S(2)}) copy-start(f32[2,1536]{1,0:T(2,128)} %param.17) | copy-start | bytes 36868
  0.7 9.2 %copy-start.11 = (f32[2,384]{1,0:T(2,128)S(1)}, f32[2,384]{1,0:T(2,128)}, u32[]{:S(2)}) copy-start(f32[2,384]{1,0:T(2,128)} %param.15) | copy-start | bytes 9220
  1.9 10.3 %collective-permute-start.1 = (bf16[3,128,384]{2,1,0:T(8,128)(2,1)S(1)}, bf16[3,128,384]{2,1,0:T(8,128)(2,1)S(1)}, u32[]{:S(2)}, u32[]{:S(2)}) collective-permute-start(bf16[3,128,384]{2,1,0:T(8,128)(2,1)S(1)} %get-tuple-element.114), channel_id=1, source_target_pairs={{1,0},{2,1},{3,2},{4,3},{5,4},{6,5},{7,6},{8,7},{9,8},{10,9},{11,1... | collective-permute-start | bytes 884744 | tf_op jit(solution)/shard_map/ppermute | solution.py:15
  4.5 7.5 %collective-permute-start = (bf16[3,128,384]{2,1,0:T(8,128)(2,1)S(1)}, bf16[3,128,384]{2,1,0:T(8,128)(2,1)S(1)}, u32[]{:S(2)}, u32[]{:S(2)}) collective-permute-start(bf16[3,128,384]{2,1,0:T(8,128)(2,1)S(1)} %get-tuple-element.115), channel_id=1, source_target_pairs={{0,1},{1,2},{2,3},{3,4},{4,5},{5,6},{6,7},{7,8},{8,9},{9,10},{10,1... | collective-permute-start | bytes 884744 | tf_op jit(solution)/shard_map/ppermute | solution.py:14
  24.6 1.9 %copy-start.2 = (f32[8,128,384]{2,1,0:T(8,128)S(1)}, f32[8,128,384]{2,1,0:T(8,128)}, u32[]{:S(2)}) copy-start(f32[8,128,384]{2,1,0:T(8,128)} %get-tuple-element.109) | copy-start | bytes 4718596
  26.5 1.7 %copy-start.13 = (bf16[2,384,1536]{2,1,0:T(8,128)(2,1)S(1)}, bf16[2,384,1536]{2,1,0:T(8,128)(2,1)}, u32[]{:S(2)}) copy-start(bf16[2,384,1536]{2,1,0:T(8,128)(2,1)} %param.16) | copy-start | bytes 7077892
  28.2 2.9 %copy-start.6 = (bf16[8,128,384]{2,1,0:T(8,128)(2,1)S(1)}, bf16[8,128,384]{2,1,0:T(8,128)(2,1)}, u32[]{:S(2)}) copy-start(bf16[8,128,384]{2,1,0:T(8,128)(2,1)} %param.12) | copy-start | bytes 2359300
  28.2 2.9 %copy-start.15 = (bf16[2,384,1536]{2,1,0:T(8,128)(2,1)S(1)}, bf16[2,384,1536]{2,1,0:T(8,128)(2,1)}, u32[]{:S(2)}) copy-start(bf16[2,384,1536]{2,1,0:T(8,128)(2,1)} %param.18) | copy-start | bytes 7077892
  31.1 2.7 %copy-start.8 = (bf16[384,256]{1,0:T(8,128)(2,1)S(1)}, bf16[384,256]{1,0:T(8,128)(2,1)}, u32[]{:S(2)}) copy-start(bf16[384,256]{1,0:T(8,128)(2,1)} %param.19) | copy-start | bytes 589828
  32.9 0.9 copy-start.7
  33.8 9.0 %copy-start.18 = (s32[16]{0:T(128)S(1)}, s32[16]{0:T(128)}, u32[]{:S(2)}) copy-start(s32[16]{0:T(128)} %param.21) | copy-start | bytes 196
  33.8 9.2 %copy-start.12 = (s32[128]{0:T(128)S(1)}, s32[128]{0:T(128)}, u32[]{:S(2)}) copy-start(s32[128]{0:T(128)} %param.22) | copy-start | bytes 1540
  35.4 21.1 %all-to-all-start = ((bf16[8,128,256]{2,0,1:T(8,128)(2,1)}), bf16[8,128,256]{2,0,1:T(8,128)(2,1)S(1)}, u32[]{:S(2)}, u32[]{:S(2)}) async-start(bf16[8,128,256]{2,0,1:T(8,128)(2,1)} %copy.37), calls=%async_computation | async-start | bytes 1048576 | tf_op jit(solution)/shard_map/all_to_all | solution.py:48
  57.2 15.0 %copy-start.10 = (s32[8,128]{1,0:T(8,128)S(1)}, s32[8,128]{1,0:T(8,128)}, u32[]{:S(2)}) copy-start(s32[8,128]{1,0:T(8,128)} %param.23) | copy-start | bytes 12292
  57.2 28.5 %copy-start.17 = (bf16[8,128,384]{2,1,0:T(8,128)(2,1)S(1)}, bf16[8,128,384]{2,1,0:T(8,128)(2,1)}, u32[]{:S(2)}) copy-start(bf16[8,128,384]{2,1,0:T(8,128)(2,1)} %param.13) | copy-start | bytes 2359300
  67.3 18.4 %all-to-all-start.1 = ((bf16[16,8,8,256]{3,2,1,0:T(8,128)(2,1)}), bf16[16,8,8,256]{3,2,1,0:T(8,128)(2,1)S(1)}, u32[]{:S(2)}, u32[]{:S(2)}) async-start(bf16[16,8,8,256]{3,2,1,0:T(8,128)(2,1)} %constant_dynamic-update-slice_fusion.3), calls=%async_computation.1 | async-start | bytes 1048576 | tf_op jit(solution)/shard_map/all_to_all | solution.py:51
  86.2 13.0 %copy-start.3 = (bf16[8,128,384]{2,1,0:T(8,128)(2,1)}, bf16[8,128,384]{2,1,0:T(8,128)(2,1)S(1)}, u32[]{:S(2)}) copy-start(bf16[8,128,384]{2,1,0:T(8,128)(2,1)S(1)} %add_convert_fusion.1) | copy-start | bytes 2359300
  86.3 7.4 %collective-permute-start.2 = (bf16[3,128,384]{2,1,0:T(8,128)(2,1)S(1)}, bf16[3,128,384]{2,1,0:T(8,128)(2,1)S(1)}, u32[]{:S(2)}, u32[]{:S(2)}) collective-permute-start(bf16[3,128,384]{2,1,0:T(8,128)(2,1)S(1)} %get-tuple-element.112), channel_id=1, source_target_pairs={{0,1},{1,2},{2,3},{3,4},{4,5},{5,6},{6,7},{7,8},{8,9},{9,10},{10,1... | collective-permute-start | bytes 884744 | tf_op jit(solution)/shard_map/ppermute | solution.py:14
  90.0 8.9 %collective-permute-start.3 = (bf16[3,128,384]{2,1,0:T(8,128)(2,1)S(1)}, bf16[3,128,384]{2,1,0:T(8,128)(2,1)S(1)}, u32[]{:S(2)}, u32[]{:S(2)}) collective-permute-start(bf16[3,128,384]{2,1,0:T(8,128)(2,1)S(1)} %get-tuple-element.113), channel_id=1, source_target_pairs={{1,0},{2,1},{3,2},{4,3},{5,4},{6,5},{7,6},{8,7},{9,8},{10,9},{11,1... | collective-permute-start | bytes 884744 | tf_op jit(solution)/shard_map/ppermute | solution.py:15
  111.2 1.9 %copy-start.1 = (f32[8,128,384]{2,1,0:T(8,128)S(1)}, f32[8,128,384]{2,1,0:T(8,128)}, u32[]{:S(2)}) copy-start(f32[8,128,384]{2,1,0:T(8,128)} %get-tuple-element.105) | copy-start | bytes 4718596
  113.1 1.7 %copy-start.14 = (bf16[2,384,1536]{2,1,0:T(8,128)(2,1)S(1)}, bf16[2,384,1536]{2,1,0:T(8,128)(2,1)}, u32[]{:S(2)}) copy-start(bf16[2,384,1536]{2,1,0:T(8,128)(2,1)} %param.16) | copy-start | bytes 7077892
  114.8 2.9 %copy-start.4 = (bf16[8,128,384]{2,1,0:T(8,128)(2,1)S(1)}, bf16[8,128,384]{2,1,0:T(8,128)(2,1)}, u32[]{:S(2)}) copy-start(bf16[8,128,384]{2,1,0:T(8,128)(2,1)} %copy-done.3) | copy-start | bytes 2359300
  114.8 2.9 %copy-start.16 = (bf16[2,384,1536]{2,1,0:T(8,128)(2,1)S(1)}, bf16[2,384,1536]{2,1,0:T(8,128)(2,1)}, u32[]{:S(2)}) copy-start(bf16[2,384,1536]{2,1,0:T(8,128)(2,1)} %param.18) | copy-start | bytes 7077892
